TPU v7x, 128 devices: a whole 4x4x4 slice. The times are simulated.
128 devices in a mesh: rep: 32 (over z, y, core), tensor: 4 (over x).
Axes of the slice: x: 4, y: 4, z: 4, core: 2. Of those that a mesh axis runs over, the one named last changes fastest.
Arguments:
- hidden_in: bfloat16 [2048, 4096], P('rep', 'tensor'), may hold values from -25 to 25
- query: bfloat16 [2048, 4096], P('rep', 'tensor'), may hold values from -6 to 6
- new_kv: bfloat16 [2048, 2, 512], P('rep', None, 'tensor'), may hold values from -8 to 8
- pool: bfloat16 [4096, 128, 2, 512], P('rep', None, None, 'tensor'), may hold values from -8 to 8
- page_table: int32 [2048, 2], P('rep'), may hold values from 0 to 127, as said below
- lengths: int32 [2048], replicated, may hold values from 1 to 256, 262144 in all
- dest: int32 [32], replicated, may hold values from 0 to 31, each once
- out_weight: bfloat16 [4096, 4096], P('tensor'), may hold values from -0.1875 to 0.1875
- norm_gain: float32 [4096], P('tensor'), may hold values from 0.1 to 1.9
- gate_up: bfloat16 [4096, 2, 11008], P('tensor', None, 'rep'), may hold values from -0.09375 to 0.09375
- down_weight: bfloat16 [11008, 4096], P('rep', 'tensor'), may hold values from -0.109375 to 0.109375
Outputs:
- layer_out: bfloat16 [2048, 4096], P('rep', 'tensor')
Inputs may be any that keep to these rules, and one draw needn't show every extreme that they name: `page_table`: within a group no two requests share a page.
All inputs are finite; a program needn't handle non-finite values.
Results may differ from a plain program's by a relative error of at most 0.03.
Values may be sent and summed in bfloat16 or wider, within the bound.
No kernel may reach another device: no remote copies, remote signals or barrier semaphores. Data moves between devices by JAX's collectives and lax.ppermute only.
A program may use at most 128 MiB of HBM per device.

v0:
```python
import jax
import jax.numpy as jnp
from jax import lax
from jax.sharding import PartitionSpec as P

D = 4096
HD = 128
EPSILON = 1e-05


def attend(queries, cache_block, new_pair, counts):
    row_count = cache_block.shape[0]
    cache_len = cache_block.shape[1]
    kv_width = cache_block.shape[3]
    kv_heads = kv_width // HD
    group_size = queries.shape[1] // kv_width
    query_heads = queries.reshape(row_count, kv_heads, group_size, HD)
    key_heads = cache_block[:, :, 0].reshape(row_count, cache_len, kv_heads, HD)
    value_heads = cache_block[:, :, 1].reshape(row_count, cache_len, kv_heads, HD)
    new_key = new_pair[:, 0].reshape(row_count, kv_heads, HD)
    new_value = new_pair[:, 1].reshape(row_count, kv_heads, HD)
    score_scale = HD ** (-0.5)
    scores = (
        jnp.einsum("nkgd,nlkd->nkgl", query_heads, key_heads, preferred_element_type=jnp.float32)
        * score_scale
    )
    own_score = (
        jnp.einsum("nkgd,nkd->nkg", query_heads, new_key, preferred_element_type=jnp.float32)
        * score_scale
    )
    in_range = (jnp.arange(cache_len, dtype=jnp.int32)[None, :] < counts[:, None])[:, None, None, :]
    masked = jnp.where(in_range, scores, -jnp.inf)
    peak_score = jnp.maximum(jnp.max(masked, axis=-1), own_score)
    weights = jnp.where(in_range, jnp.exp(scores - peak_score[..., None]), 0.0)
    own_weight = jnp.exp(own_score - peak_score)
    denominator = jnp.sum(weights, axis=-1) + own_weight
    weighted = jnp.einsum(
        "nkgl,nlkd->nkgd",
        weights.astype(jnp.bfloat16),
        value_heads,
        preferred_element_type=jnp.float32,
    )
    weighted = weighted + jnp.einsum(
        "nkg,nkd->nkgd",
        own_weight.astype(jnp.bfloat16),
        new_value,
        preferred_element_type=jnp.float32,
    )
    return (weighted / denominator[..., None]).astype(jnp.bfloat16).reshape(row_count, -1)


def local(
    hidden_in,
    query,
    new_kv,
    pool,
    page_table,
    lengths,
    dest,
    out_weight,
    norm_gain,
    gate_up,
    down_weight,
):
    rows_here = hidden_in.shape[0]
    group_count = lax.axis_size("rep")
    my_group = lax.axis_index("rep")
    group_ids = jnp.arange(group_count, dtype=jnp.int32)
    source = jnp.sum(jnp.where(dest == my_group, group_ids, 0))
    page_count = page_table.shape[1]
    page_len = pool.shape[1]
    kv_width = pool.shape[3]
    cache_rows = pool[page_table].reshape(rows_here, page_count * page_len, 2, kv_width)
    my_lengths = lax.dynamic_slice_in_dim(lengths, my_group * rows_here, rows_here)
    home_attn = attend(query, cache_rows, new_kv, my_lengths)
    every_attn, every_hidden = (
        lax.all_gather(home_attn[-1:], "rep", axis=0, tiled=True),
        lax.all_gather(hidden_in[-1:], "rep", axis=0, tiled=True),
    )
    attention = jnp.concatenate(
        [home_attn[:-1], lax.dynamic_slice_in_dim(every_attn, source, 1)], axis=0
    )
    served = jnp.concatenate(
        [hidden_in[:-1], lax.dynamic_slice_in_dim(every_hidden, source, 1)], axis=0
    )
    projected = jnp.dot(attention, out_weight, preferred_element_type=jnp.float32)
    head_total = lax.psum_scatter(
        projected.astype(jnp.bfloat16), "tensor", scatter_dimension=1, tiled=True
    ).astype(jnp.float32)
    residual = served.astype(jnp.float32) + head_total
    square_sum = lax.psum(jnp.sum(residual * residual, axis=1), "tensor")
    normed = (residual * lax.rsqrt(square_sum / D + EPSILON)[:, None] * norm_gain[None, :]).astype(
        jnp.bfloat16
    )
    unit_count = gate_up.shape[2]
    flat_weight = gate_up.reshape(gate_up.shape[0], 2 * unit_count)
    partial_units = jnp.dot(
        lax.all_gather(normed, "rep", axis=0, tiled=True),
        flat_weight,
        preferred_element_type=jnp.float32,
    )
    partial_units = partial_units.reshape(partial_units.shape[0], 2, unit_count)
    unit_total = lax.psum(partial_units.astype(jnp.bfloat16), "tensor").astype(jnp.float32)
    activated = (jax.nn.silu(unit_total[:, 0]) * unit_total[:, 1]).astype(jnp.bfloat16)
    mixed = lax.psum_scatter(
        jnp.dot(activated, down_weight, preferred_element_type=jnp.float32).astype(jnp.bfloat16),
        "rep",
        scatter_dimension=0,
        tiled=True,
    ).astype(jnp.float32)
    return (residual + mixed).astype(jnp.bfloat16)


def solution(mesh):
    return jax.shard_map(
        local,
        mesh=mesh,
        in_specs=(
            P("rep", "tensor"),
            P("rep", "tensor"),
            P("rep", None, "tensor"),
            P("rep", None, None, "tensor"),
            P("rep", None),
            P(),
            P(),
            P("tensor", None),
            P("tensor"),
            P("tensor", None, "rep"),
            P("rep", "tensor"),
        ),
        out_specs=P("rep", "tensor"),
        check_vma=False,
    )
```

profile of v0, /device:TPU:0, one launch (start us, length us, event | category | flops | bytes accessed | tf_op | source)
XLA Modules:
  0.0 336.0 jit_solution(7279921076718886438)
XLA Ops:
  6.5 0.0 copy-start
  6.5 0.0 reduce-scatter.3.cloned.1.call-start
  6.5 0.8 compare_select_fusion
  7.3 0.1 copy.17
  7.4 0.1 reshape.104
  7.6 23.2 %gather_fusion = bf16[128,128,2,128]{3,2,1,0:T(2,128)(2,1)} fusion(bf16[128,128,2,128]{3,2,1,0:T(2,128)(2,1)} %param.14, s32[1024]{0:T(1024)S(1)} %pad_clamp_fusion), kind=kCustom, calls=%fused_computation | custom fusion | bytes 16777728 | tf_op jit(solution)/shard_map/gather | solution.py:73
  30.8 0.0 copy-start.3
  30.8 0.0 copy-start.4
  30.8 8.9 %copy.18 = bf16[128,128,2,128]{3,1,0,2:T(8,128)(2,1)} copy(bf16[128,128,2,128]{3,2,1,0:T(2,128)(2,1)} %gather_fusion) | data formatting | bytes 16777216 | tf_op jit(solution)/shard_map/gather | solution.py:73
  39.7 0.8 dynamic_slice.10
  40.4 0.1 iota_compare_fusion
  40.5 0.0 copy-done.3
  40.5 0.0 copy-done.4
  40.6 0.2 fusion.22
  40.8 3.5 %select_reduce_fusion = (f32[64,8]{1,0:T(8,128)S(1)}, f32[64,256,8]{1,2,0:T(8,128)S(1)}) fusion(pred[64,256]{1,0:T(8,128)(4,1)S(1)} %iota_compare_fusion, bf16[64,8,128]{2,1,0:T(8,128)(2,1)S(1)} %bitcast.79, bf16[64,256,2,128]{3,1,0,2:T(8,128)(2,1)} %bitcast.68), kind=kOutput, calls=%fused_computation.23 | convolution fusion | flops 33947136 | bytes 4868096 | tf_op jit(solution)/shard_map/nkgd,nlkd->nkgl/dot_general | solution.py:24
  44.3 0.0 copy-start.7
  44.3 0.3 bitcast_reduce_fusion
  44.6 2.9 fusion.15
  47.5 26.2 %all-gather.1 = bf16[32,1,1024]{2,1,0:T(2,128)(2,1)S(1)} all-gather(bf16[1,1,1024]{2,1,0:T(2,128)(2,1)S(1)} %reshape.115), channel_id=1, replica_groups=mesh['rep'=32,'tensor'=4] {'rep'}, dimensions={0}, use_global_device_ids=true | all-gather | bytes 67584 | tf_op jit(solution)/shard_map/all_gather | solution.py:77
  73.7 0.0 copy-done.7
  73.7 0.6 fusion.25
  76.4 0.0 copy-start.1
  76.4 0.0 copy-start.5
  76.4 5.8 %convolution_convert_fusion = bf16[64,4096]{1,0:T(8,128)(2,1)} fusion(bf16[1024,4096]{1,0:T(8,128)(2,1)} %param.18, bf16[1,1024]{1,0:T(2,128)(2,1)S(1)} %dynamic-slice_bitcast_fusion, bf16[63,1024]{1,0:T(8,128)(2,1)S(1)} %bitcast.73), kind=kOutput, calls=%fused_computation.1 | convolution fusion | flops 537395200 | bytes 9043968 | tf_op jit(solution)/shard_map/dot_general | solution.py:86
  82.2 0.0 reduce-scatter.3.cloned.1.call-update
  82.2 0.0 all-gather.4.cloned.1.call-start
  82.2 0.0 copy-done.1
  82.3 24.0 %all-gather = bf16[32,1,1024]{2,1,0:T(2,128)(2,1)S(1)} all-gather(bf16[1,1,1024]{2,1,0:T(2,128)(2,1)S(1)} %slice_bitcast_fusion.14), channel_id=1, replica_groups=mesh['rep'=32,'tensor'=4] {'rep'}, dimensions={0}, use_global_device_ids=true | all-gather | bytes 67584 | tf_op jit(solution)/shard_map/all_gather | solution.py:78
  106.3 0.0 reduce-scatter.3.cloned.1.call-done
  106.3 1.1 multiply_reduce_fusion
  107.4 10.5 %psum.14 = f32[64]{0:T(128)S(1)} all-reduce(f32[64]{0:T(128)S(1)} %multiply_reduce_fusion), channel_id=1, replica_groups=mesh['rep'=32,'tensor'=4] {'tensor'}, use_global_device_ids=true, to_apply=%region_5.6 | all-reduce | flops 64 | bytes 512 | tf_op jit(solution)/shard_map/psum | solution.py:91
  117.9 0.0 copy-done.5
  117.9 1.7 multiply_convert_fusion
  119.6 0.0 all-gather.4.cloned.1.call-update
  119.6 0.0 all-reduce.2.cloned.1.call-start
  119.6 42.7 %all-gather.4.cloned.1.call-done = bf16[2048,1024]{1,0:T(8,128)(2,1)} async-done(((bf16[64,1024]{1,0:T(8,128)(2,1)}), bf16[2048,1024]{1,0:T(8,128)(2,1)}) %all-gather.4.cloned.1.call-update) | async-done | bytes 4194320 | tf_op jit(solution)/shard_map/all_gather | solution.py:98
  162.3 0.0 copy-done
  162.3 6.7 %fusion.4 = bf16[2048,2,344]{0,2,1:T(8,128)(2,1)} fusion(bf16[2048,1024]{1,0:T(8,128)(2,1)} %all-gather.4.cloned.1.call-done, bf16[1024,2,344]{0,2,1:T(8,128)(2,1)S(1)} %copy-done), kind=kOutput, calls=%fused_computation.9 | convolution fusion | flops 2887090176 | bytes 8421376 | tf_op jit(solution)/shard_map/dot_general | solution.py:97
  169.0 0.0 all-reduce.2.cloned.1.call-update
  169.0 0.0 copy-start.6
  169.0 0.2 reduce-scatter.5.cloned.1.call-start
  169.3 69.5 %all-reduce.2.cloned.1.call-done = bf16[2048,2,344]{0,2,1:T(8,128)(2,1)} async-done(((bf16[2048,2,344]{0,2,1:T(8,128)(2,1)}), bf16[2048,2,344]{0,2,1:T(8,128)(2,1)}) %all-reduce.2.cloned.1.call-update) | async-done | bytes 2818064 | tf_op jit(solution)/shard_map/psum | solution.py:103
  238.8 2.5 convert_element_type.50
  241.3 0.0 copy-done.6
  241.3 4.4 %convolution_convert_fusion.1 = bf16[2048,1024]{1,0:T(8,128)(2,1)} fusion(bf16[344,1024]{1,0:T(8,128)(2,1)S(1)} %copy-done.6, f32[2048,2,344]{0,2,1:T(8,128)S(1)} %convert_element_type.50), kind=kOutput, calls=%fused_computation.8 | convolution fusion | flops 1449164800 | bytes 10534912 | tf_op jit(solution)/shard_map/dot_general | solution.py:106
  245.8 0.0 copy-start.2
  245.8 0.0 reduce-scatter.5.cloned.1.call-update
  245.8 82.1 %reduce-scatter.5.cloned.1.call-done = bf16[64,1024]{1,0:T(8,128)(2,1)} async-done(((bf16[2048,1024]{1,0:T(8,128)(2,1)}), bf16[64,1024]{1,0:T(8,128)(2,1)}) %reduce-scatter.5.cloned.1.call-update) | async-done | bytes 131088 | tf_op jit(solution)/shard_map/reduce_scatter | solution.py:105
  327.9 0.0 copy-done.2
  327.9 1.6 add_convert_fusion
  (15 shorter events, 0.2 us)
Async XLA Ops:
  6.5 155.8 %copy-start = (bf16[1024,2,344]{0,2,1:T(8,128)(2,1)S(1)}, bf16[1024,2,344]{0,2,1:T(8,128)(2,1)}, u32[]{:S(2)}) copy-start(bf16[1024,2,344]{0,2,1:T(8,128)(2,1)} %param.20) | copy-start | bytes 4227076
  6.5 99.8 %reduce-scatter.3.cloned.1.call-start = ((), (), s32[]{:S(2)}) async-start(), calls=%async_computation.2 | async-start | bytes 655360 | tf_op jit(solution)/shard_map/reduce_scatter | solution.py:87
  30.8 9.7 %copy-start.3 = (bf16[64,1024]{1,0:T(8,128)(2,1)S(1)}, bf16[64,1024]{1,0:T(8,128)(2,1)}, u32[]{:S(2)}) copy-start(bf16[64,1024]{1,0:T(8,128)(2,1)} %param.12) | copy-start | bytes 393220
  30.8 9.8 %copy-start.4 = (bf16[64,2,128]{2,1,0:T(2,128)(2,1)S(1)}, bf16[64,2,128]{2,1,0:T(2,128)(2,1)}, u32[]{:S(2)}) copy-start(bf16[64,2,128]{2,1,0:T(2,128)(2,1)} %param.13) | copy-start | bytes 98308
  44.3 29.4 %copy-start.7 = (s32[32]{0:T(128)S(1)}, s32[32]{0:T(128)}, u32[]{:S(2)}) copy-start(s32[32]{0:T(128)} %param.17) | copy-start | bytes 388
  76.4 5.9 %copy-start.1 = (bf16[64,1024]{1,0:T(8,128)(2,1)S(1)}, bf16[64,1024]{1,0:T(8,128)(2,1)}, u32[]{:S(2)}) copy-start(bf16[64,1024]{1,0:T(8,128)(2,1)} %param.11) | copy-start | bytes 393220
  76.4 41.5 %copy-start.5 = (f32[1024]{0:T(1024)S(1)}, f32[1024]{0:T(1024)}, u32[]{:S(2)}) copy-start(f32[1024]{0:T(1024)} %param.19) | copy-start | bytes 12292
  82.2 80.1 %all-gather.4.cloned.1.call-start = ((), (), s32[]{:S(2)}) async-start(), calls=%async_computation.3 | async-start | bytes 4325376 | tf_op jit(solution)/shard_map/all_gather | solution.py:98
  119.6 119.2 %all-reduce.2.cloned.1.call-start = ((), (), s32[]{:S(2)}) async-start(), calls=%async_computation.4 | async-start | bytes 5636096 | tf_op jit(solution)/shard_map/psum | solution.py:103
  169.0 72.3 %copy-start.6 = (bf16[344,1024]{1,0:T(8,128)(2,1)S(1)}, bf16[344,1024]{1,0:T(8,128)(2,1)}, u32[]{:S(2)}) copy-start(bf16[344,1024]{1,0:T(8,128)(2,1)} %param.21) | copy-start | bytes 2113540
  169.0 158.8 %reduce-scatter.5.cloned.1.call-start = ((), (), s32[]{:S(2)}) async-start(), calls=%async_computation.5 | async-start | bytes 4325376 | tf_op jit(solution)/shard_map/reduce_scatter | solution.py:105
  245.8 82.1 %copy-start.2 = (bf16[64,1024]{1,0:T(8,128)(2,1)S(1)}, bf16[64,1024]{1,0:T(8,128)(2,1)}, u32[]{:S(2)}) copy-start(bf16[64,1024]{1,0:T(8,128)(2,1)} %reduce-scatter.3.cloned.1.call-done) | copy-start | bytes 393220
Sparse Core Ops, SparseCore 0:
  82.3 20.4 reduce-scatter.2
  119.7 42.5 all-gather.3
  169.1 69.5 all-reduce.1
  245.9 81.9 reduce-scatter.4
where the time goes:
time: 336 us
  waiting for transfers between devices  194 us (58%)
  blocking collectives  60.7 us (18%)
  local copies, waits for them, and re-layouts  33.2 us (10%)
  matrix products  23.4 us (7%)
  between operations  15.3 us (5%)
  other arithmetic  8.71 us (3%)
    reduce_scatter x1, waiting for transfers between devices, local(): lax.psum_scatter(jnp.dot(activated, down_weight, preferred_element_type=j...  82.1 us
    psum x1, waiting for transfers between devices, local(): lax.psum(partial_units.astype(jnp.bfloat16), 'tensor').astype(jnp.float32)  69.5 us
    all_gather x1, waiting for transfers between devices, local(): lax.all_gather(normed, 'rep', axis=0, tiled=True)  42.7 us
    gather x2, local copies, waits for them, and re-layouts, local(): pool[page_table].reshape(rows_here, page_count * page_len, 2, kv_width)  32.1 us
    all_gather x1, blocking collectives, local(): lax.all_gather(home_attn[-1:], 'rep', axis=0, tiled=True)  26.2 us
    all_gather x1, blocking collectives, local(): lax.all_gather(hidden_in[-1:], 'rep', axis=0, tiled=True)  24 us
    psum x1, blocking collectives, local(): square_sum = lax.psum(jnp.sum(residual * residual, axis=1), 'tensor')  10.5 us
  transfers between devices with their start and end apart: 4, of which 3 were waited for; matrix products, arithmetic and copies ran while one was open for 0% of the time, Pallas kernels for 0%

commit v1 on v0

--- a/solution.py
+++ b/solution.py
@@ -6,6 +6,12 @@
 D = 4096
 HD = 128
 EPSILON = 1e-05
+
+
+def open_the_roots(a0, axis_id):
+    return jnp.concatenate(
+        lax.all_to_all(jnp.stack([a0] * lax.axis_size(axis_id)), axis_id, 0, 0), axis=0
+    )
 
 
 def attend(queries, cache_block, new_pair, counts):
@@ -74,7 +80,7 @@
     my_lengths = lax.dynamic_slice_in_dim(lengths, my_group * rows_here, rows_here)
     home_attn = attend(query, cache_rows, new_kv, my_lengths)
     every_attn, every_hidden = (
-        lax.all_gather(home_attn[-1:], "rep", axis=0, tiled=True),
+        open_the_roots(home_attn[-1:], "rep"),
         lax.all_gather(hidden_in[-1:], "rep", axis=0, tiled=True),
     )
     attention = jnp.concatenate(

time: 336 us -> 325 us (0.967)
  blocking collectives: 60.7 us -> 33.3 us
  starting transfers between devices: 0.31 us -> 8.76 us
  waiting for transfers between devices: 194 us -> 199 us
    all_gather x1 -> x0, blocking collectives: 26.2 us -> none  [local(): lax.all_gather(home_attn[-1:], 'rep', axis=0, tiled=True)]
    all_to_all x0 -> x1, starting transfers between devices: none -> 8.41 us  [open_the_roots(): lax.all_to_all(jnp.stack([a0] * lax.axis_size(axis_id)), axis_id, 0, 0)]
    all_to_all x0 -> x1, waiting for transfers between devices: none -> 4.57 us  [open_the_roots(): lax.all_to_all(jnp.stack([a0] * lax.axis_size(axis_id)), axis_id, 0, 0)]
  transfers between devices with their start and end apart: 4 -> 5, of which waited for: 3 -> 4; matrix products, arithmetic and copies ran while one was open for 0% -> 0% of each run, Pallas kernels for 0% -> 0%
where the time goes in v1:
time: 325 us; the launch traced here: 324 us
  waiting for transfers between devices  199 us (61%)
  local copies, waits for them, and re-layouts  34.5 us (11%)
  blocking collectives  33.3 us (10%)
  matrix products  23.4 us (7%)
  between operations  15.4 us (5%)
  other arithmetic  9.8 us (3%)
  starting transfers between devices  8.76 us (3%)
    reduce_scatter x1, waiting for transfers between devices, local(): lax.psum_scatter(jnp.dot(activated, down_weight, preferred_element_type=j...  82.1 us
    psum x1, waiting for transfers between devices, local(): lax.psum(partial_units.astype(jnp.bfloat16), 'tensor').astype(jnp.float32)  69.5 us
    all_gather x1, waiting for transfers between devices, local(): lax.all_gather(normed, 'rep', axis=0, tiled=True)  43 us
    gather x2, local copies, waits for them, and re-layouts, local(): pool[page_table].reshape(rows_here, page_count * page_len, 2, kv_width)  32.1 us
    all_gather x1, blocking collectives, local(): lax.all_gather(hidden_in[-1:], 'rep', axis=0, tiled=True)  22.8 us
    psum x1, blocking collectives, local(): square_sum = lax.psum(jnp.sum(residual * residual, axis=1), 'tensor')  10.5 us
    all_to_all x1, starting transfers between devices, open_the_roots(): lax.all_to_all(jnp.stack([a0] * lax.axis_size(axis_id)), axis_id, 0, 0)  8.41 us
    dot_general x1, matrix products, local(): jnp.dot(lax.all_gather(normed, 'rep', axis=0, tiled=True), flat_weight, p...  6.65 us
  transfers between devices with their start and end apart: 5, of which 4 were waited for; matrix products, arithmetic and copies ran while one was open for 0% of the time, Pallas kernels for 0%

profile of v1, /device:TPU:0, one launch (start us, length us, event | category | flops | bytes accessed | tf_op | source)
XLA Modules:
  0.0 324.4 jit_solution(13798632474212014526)
XLA Ops:
  6.5 0.0 copy-start
  6.5 0.8 compare_select_fusion
  7.3 0.1 copy.17
  7.4 0.1 reshape.111
  7.6 23.2 %gather_fusion = bf16[128,128,2,128]{3,2,1,0:T(2,128)(2,1)} fusion(bf16[128,128,2,128]{3,2,1,0:T(2,128)(2,1)} %param.14, s32[1024]{0:T(1024)S(1)} %pad_clamp_fusion), kind=kCustom, calls=%fused_computation | custom fusion | bytes 16777728 | tf_op jit(solution)/shard_map/gather | solution.py:79
  30.8 0.0 copy-start.3
  30.8 0.0 copy-start.4
  30.8 8.9 %copy.18 = bf16[128,128,2,128]{3,1,0,2:T(8,128)(2,1)} copy(bf16[128,128,2,128]{3,2,1,0:T(2,128)(2,1)} %gather_fusion) | data formatting | bytes 16777216 | tf_op jit(solution)/shard_map/gather | solution.py:79
  39.7 0.8 dynamic_slice.12
  40.4 0.1 iota_compare_fusion
  40.5 0.0 copy-done.3
  40.5 0.0 copy-done.4
  40.6 0.2 fusion.22
  40.8 3.5 %select_reduce_fusion = (f32[64,8]{1,0:T(8,128)S(1)}, f32[64,256,8]{1,2,0:T(8,128)S(1)}) fusion(pred[64,256]{1,0:T(8,128)(4,1)S(1)} %iota_compare_fusion, bf16[64,8,128]{2,1,0:T(8,128)(2,1)S(1)} %bitcast.81, bf16[64,256,2,128]{3,1,0,2:T(8,128)(2,1)} %bitcast.70), kind=kOutput, calls=%fused_computation.23 | convolution fusion | flops 33947136 | bytes 4868096 | tf_op jit(solution)/shard_map/nkgd,nlkd->nkgl/dot_general | solution.py:30
  44.3 0.0 copy-start.7
  44.3 0.3 bitcast_reduce_fusion
  44.6 2.9 fusion.15
  47.5 0.1 stack.5
  47.6 0.5 broadcast.44
  48.1 1.0 reduce.5
  49.1 0.7 reshape.126
  49.8 8.4 %all-to-all-start = ((bf16[32,2,512]{2,1,0:T(2,128)(2,1)}), bf16[32,2,512]{2,1,0:T(2,128)(2,1)S(1)}, u32[]{:S(2)}, u32[]{:S(2)}) async-start(bf16[32,2,512]{2,1,0:T(2,128)(2,1)} %reshape.126), calls=%async_computation | async-start | bytes 131072 | tf_op jit(solution)/shard_map/all_to_all | solution.py:13
  58.2 0.0 reduce-scatter.3.cloned.1.call-start
  58.3 0.0 copy-done.7
  58.3 0.7 fusion.25
  61.1 4.6 %all-to-all-done = bf16[32,2,512]{2,1,0:T(2,128)(2,1)S(1)} async-done(((bf16[32,2,512]{2,1,0:T(2,128)(2,1)}), bf16[32,2,512]{2,1,0:T(2,128)(2,1)S(1)}, u32[]{:S(2)}, u32[]{:S(2)}) %all-to-all-start) | async-done | bytes 65568 | tf_op jit(solution)/shard_map/all_to_all | solution.py:13
  65.7 0.1 reshape.127
  65.8 0.0 copy-start.1
  65.8 0.0 copy-start.5
  65.8 5.8 %convolution_convert_fusion = bf16[64,4096]{1,0:T(8,128)(2,1)} fusion(bf16[1024,4096]{1,0:T(8,128)(2,1)} %param.18, bf16[1,1024]{1,0:T(2,128)(2,1)S(1)} %dynamic-slice_bitcast_fusion.1, bf16[63,1024]{1,0:T(8,128)(2,1)S(1)} %bitcast.75), kind=kOutput, calls=%fused_computation.1 | convolution fusion | flops 537395200 | bytes 9043968 | tf_op jit(solution)/shard_map/dot_general | solution.py:92
  71.6 0.0 reduce-scatter.3.cloned.1.call-update
  71.6 0.0 all-gather.3.cloned.1.call-start
  71.6 0.0 copy-done.1
  71.7 22.8 %all-gather = bf16[32,1,1024]{2,1,0:T(2,128)(2,1)S(1)} all-gather(bf16[1,1,1024]{2,1,0:T(2,128)(2,1)S(1)} %slice_bitcast_fusion.14), channel_id=1, replica_groups=mesh['rep'=32,'tensor'=4] {'rep'}, dimensions={0}, use_global_device_ids=true | all-gather | bytes 67584 | tf_op jit(solution)/shard_map/all_gather | solution.py:84
  94.4 0.0 reduce-scatter.3.cloned.1.call-done
  94.4 1.1 multiply_reduce_fusion
  95.5 10.5 %psum.14 = f32[64]{0:T(128)S(1)} all-reduce(f32[64]{0:T(128)S(1)} %multiply_reduce_fusion), channel_id=1, replica_groups=mesh['rep'=32,'tensor'=4] {'tensor'}, use_global_device_ids=true, to_apply=%region_5.6 | all-reduce | flops 64 | bytes 512 | tf_op jit(solution)/shard_map/psum | solution.py:97
  106.0 0.0 copy-done.5
  106.0 1.7 multiply_convert_fusion
  107.7 0.0 all-gather.3.cloned.1.call-update
  107.7 0.0 all-reduce.2.cloned.1.call-start
  107.7 43.0 %all-gather.3.cloned.1.call-done = bf16[2048,1024]{1,0:T(8,128)(2,1)} async-done(((bf16[64,1024]{1,0:T(8,128)(2,1)}), bf16[2048,1024]{1,0:T(8,128)(2,1)}) %all-gather.3.cloned.1.call-update) | async-done | bytes 4194320 | tf_op jit(solution)/shard_map/all_gather | solution.py:104
  150.7 0.0 copy-done
  150.7 6.6 %fusion.4 = bf16[2048,2,344]{0,2,1:T(8,128)(2,1)} fusion(bf16[2048,1024]{1,0:T(8,128)(2,1)} %all-gather.3.cloned.1.call-done, bf16[1024,2,344]{0,2,1:T(8,128)(2,1)S(1)} %copy-done), kind=kOutput, calls=%fused_computation.9 | convolution fusion | flops 2887090176 | bytes 8421376 | tf_op jit(solution)/shard_map/dot_general | solution.py:103
  157.4 0.0 all-reduce.2.cloned.1.call-update
  157.4 0.0 copy-start.6
  157.4 0.2 reduce-scatter.5.cloned.1.call-start
  157.6 69.5 %all-reduce.2.cloned.1.call-done = bf16[2048,2,344]{0,2,1:T(8,128)(2,1)} async-done(((bf16[2048,2,344]{0,2,1:T(8,128)(2,1)}), bf16[2048,2,344]{0,2,1:T(8,128)(2,1)}) %all-reduce.2.cloned.1.call-update) | async-done | bytes 2818064 | tf_op jit(solution)/shard_map/psum | solution.py:109
  227.2 2.5 convert_element_type.50
  229.7 0.0 copy-done.6
  229.7 4.4 %convolution_convert_fusion.1 = bf16[2048,1024]{1,0:T(8,128)(2,1)} fusion(bf16[344,1024]{1,0:T(8,128)(2,1)S(1)} %copy-done.6, f32[2048,2,344]{0,2,1:T(8,128)S(1)} %convert_element_type.50), kind=kOutput, calls=%fused_computation.8 | convolution fusion | flops 1449164800 | bytes 10534912 | tf_op jit(solution)/shard_map/dot_general | solution.py:112
  234.2 0.0 copy-start.2
  234.2 0.0 reduce-scatter.5.cloned.1.call-update
  234.2 82.1 %reduce-scatter.5.cloned.1.call-done = bf16[64,1024]{1,0:T(8,128)(2,1)} async-done(((bf16[2048,1024]{1,0:T(8,128)(2,1)}), bf16[64,1024]{1,0:T(8,128)(2,1)}) %reduce-scatter.5.cloned.1.call-update) | async-done | bytes 131088 | tf_op jit(solution)/shard_map/reduce_scatter | solution.py:111
  316.3 0.0 copy-done.2
  316.3 1.6 add_convert_fusion
  (14 shorter events, 0.2 us)
Async XLA Ops:
  6.5 144.2 %copy-start = (bf16[1024,2,344]{0,2,1:T(8,128)(2,1)S(1)}, bf16[1024,2,344]{0,2,1:T(8,128)(2,1)}, u32[]{:S(2)}) copy-start(bf16[1024,2,344]{0,2,1:T(8,128)(2,1)} %param.20) | copy-start | bytes 4227076
  30.8 9.7 %copy-start.3 = (bf16[64,1024]{1,0:T(8,128)(2,1)S(1)}, bf16[64,1024]{1,0:T(8,128)(2,1)}, u32[]{:S(2)}) copy-start(bf16[64,1024]{1,0:T(8,128)(2,1)} %param.12) | copy-start | bytes 393220
  30.8 9.8 %copy-start.4 = (bf16[64,2,128]{2,1,0:T(2,128)(2,1)S(1)}, bf16[64,2,128]{2,1,0:T(2,128)(2,1)}, u32[]{:S(2)}) copy-start(bf16[64,2,128]{2,1,0:T(2,128)(2,1)} %param.13) | copy-start | bytes 98308
  44.3 14.0 %copy-start.7 = (s32[32]{0:T(128)S(1)}, s32[32]{0:T(128)}, u32[]{:S(2)}) copy-start(s32[32]{0:T(128)} %param.17) | copy-start | bytes 388
  49.8 15.9 %all-to-all-start = ((bf16[32,2,512]{2,1,0:T(2,128)(2,1)}), bf16[32,2,512]{2,1,0:T(2,128)(2,1)S(1)}, u32[]{:S(2)}, u32[]{:S(2)}) async-start(bf16[32,2,512]{2,1,0:T(2,128)(2,1)} %reshape.126), calls=%async_computation | async-start | bytes 131072 | tf_op jit(solution)/shard_map/all_to_all | solution.py:13
  58.2 36.2 %reduce-scatter.3.cloned.1.call-start = ((), (), s32[]{:S(2)}) async-start(), calls=%async_computation.3 | async-start | bytes 655360 | tf_op jit(solution)/shard_map/reduce_scatter | solution.py:93
  65.8 5.9 %copy-start.1 = (bf16[64,1024]{1,0:T(8,128)(2,1)S(1)}, bf16[64,1024]{1,0:T(8,128)(2,1)}, u32[]{:S(2)}) copy-start(bf16[64,1024]{1,0:T(8,128)(2,1)} %param.11) | copy-start | bytes 393220
  65.8 40.2 %copy-start.5 = (f32[1024]{0:T(1024)S(1)}, f32[1024]{0:T(1024)}, u32[]{:S(2)}) copy-start(f32[1024]{0:T(1024)} %param.19) | copy-start | bytes 12292
  71.6 79.1 %all-gather.3.cloned.1.call-start = ((), (), s32[]{:S(2)}) async-start(), calls=%async_computation.4 | async-start | bytes 4325376 | tf_op jit(solution)/shard_map/all_gather | solution.py:104
  107.7 119.5 %all-reduce.2.cloned.1.call-start = ((), (), s32[]{:S(2)}) async-start(), calls=%async_computation.5 | async-start | bytes 5636096 | tf_op jit(solution)/shard_map/psum | solution.py:109
  157.4 72.3 %copy-start.6 = (bf16[344,1024]{1,0:T(8,128)(2,1)S(1)}, bf16[344,1024]{1,0:T(8,128)(2,1)}, u32[]{:S(2)}) copy-start(bf16[344,1024]{1,0:T(8,128)(2,1)} %param.21) | copy-start | bytes 2113540
  157.4 158.9 %reduce-scatter.5.cloned.1.call-start = ((), (), s32[]{:S(2)}) async-start(), calls=%async_computation.6 | async-start | bytes 4325376 | tf_op jit(solution)/shard_map/reduce_scatter | solution.py:111
  234.2 82.1 %copy-start.2 = (bf16[64,1024]{1,0:T(8,128)(2,1)S(1)}, bf16[64,1024]{1,0:T(8,128)(2,1)}, u32[]{:S(2)}) copy-start(bf16[64,1024]{1,0:T(8,128)(2,1)} %reduce-scatter.3.cloned.1.call-done) | copy-start | bytes 393220
Sparse Core Ops, SparseCore 0:
  71.7 19.0 reduce-scatter.2
  107.8 42.8 all-gather.2
  157.5 69.6 all-reduce.1
  234.3 81.9 reduce-scatter.4
